TPU v7x, 128 devices: a whole 4x4x4 slice. The times are simulated.
128 devices in a mesh: req: 8 (over x, core), mlp: 16 (over z, y).
Axes of the slice: x: 4, y: 4, z: 4, core: 2. Of those that a mesh axis runs over, the one named last changes fastest.
Arguments:
- tokens: bfloat16 [8192, 4096], P(('req', 'mlp')), may hold values from -6 to 6
- layer_norm_gain: float32 [4096], replicated, may hold values from 0.1 to 1.9
- layer_norm_bias: float32 [4096], replicated, may hold values from -2 to 2
- query_key_weight: bfloat16 [4096, 16, 768], P(None, 'mlp')
- output_weight: bfloat16 [16, 256, 4096], P('mlp'), may hold values from -0.09375 to 0.09375
- up_weight: bfloat16 [4096, 8192], P(None, 'mlp'), may hold values from -0.09375 to 0.09375
- input_bias: float32 [8192], P('mlp'), may hold values from -3 to 3
- down_weight: bfloat16 [8192, 4096], P('mlp'), may hold values from -0.0625 to 0.0625
- output_bias: float32 [4096], replicated, may hold values from -2 to 2
- input_adapter_left: bfloat16 [4096, 2048], P(None, 'mlp'), may hold values from -0.09375 to 0.09375
- query_key_value_right: bfloat16 [1024, 16, 768], P(None, 'mlp'), may hold values from -1.5 to 1.5
- up_adapter_right: bfloat16 [1024, 8192], P(None, 'mlp'), may hold values from -1.5 to 1.5
- output_adapter_left: bfloat16 [16, 256, 1024], P('mlp'), may hold values from -0.09375 to 0.09375
- down_adapter_left: bfloat16 [8192, 1024], P('mlp'), may hold values from -0.0625 to 0.0625
- output_adapter_right: bfloat16 [2048, 4096], P('mlp'), may hold values from -1 to 1
- lengths: int32 [257], replicated, may hold values from 8 to 4096, as said below
- request_adapter: int32 [257], replicated, may hold values from 0 to 63
- slot_adapter: int32 [64], P('mlp'), may hold values from 0 to 63, each once
Outputs:
- mixed: bfloat16 [8192, 4096], P(('req', 'mlp'))
Inputs may be any that keep to these rules, and one draw needn't show every extreme that they name: `lengths`: one request holds exactly 4096 tokens, every other one 8 to 24; together they hold 8192 tokens. `slot_adapter`: every adapter id stands in exactly one slot.
All inputs are finite; a program needn't handle non-finite values.
Results may differ from a plain program's by a relative error of at most 0.017.
Values may be sent and summed in bfloat16 or wider, within the bound.
A program may use at most 128 MiB of HBM per device.

v0:
```python
import math
import jax
import jax.numpy as jnp
from jax import lax
from jax.sharding import PartitionSpec as P

HEAD_SIZE = 256
ROT = 64
ADAPTER_RANK = 16
ADP_DEV = 4
EPSILON = 1e-05
NEGATIVE_FILL = -1e30


def rank_product(left_side, right_side):
    return jnp.dot(left_side, right_side, preferred_element_type=jnp.float32)


def normalize(inputs, layer_norm_gain, layer_norm_bias):
    values = inputs.astype(jnp.float32)
    center = values - jnp.mean(values, axis=1, keepdims=True)
    spread = jnp.mean(center * center, axis=1, keepdims=True)
    scaled = center * lax.rsqrt(spread + EPSILON)
    return (scaled * layer_norm_gain + layer_norm_bias).astype(jnp.bfloat16)


def token_info(lengths, request_adapter, first_row, row_count):
    endings = jnp.cumsum(lengths)
    anchors = endings - lengths
    token_index = first_row + lax.iota(jnp.int32, row_count)
    inside = anchors[None, :] <= token_index[:, None]
    request = jnp.sum(inside.astype(jnp.int32), axis=1) - 1
    request_start = jnp.max(jnp.where(inside, anchors[None, :], jnp.zeros((), jnp.int32)), axis=1)
    adapter_id = jnp.take(request_adapter, jnp.maximum(request, 0))
    return (token_index, request, token_index - request_start, adapter_id)


def rotate(matrix, position):
    row_count = matrix.shape[0]
    head_count = matrix.shape[1]
    half_rot = ROT // 2
    frequency = jnp.exp(jnp.arange(half_rot, dtype=jnp.float32) * (-2.0 * math.log(10000.0) / ROT))
    angles = position.astype(jnp.float32)[:, None] * frequency[None, :]
    cosine = jnp.cos(angles)[:, None, :]
    sine_value = jnp.sin(angles)[:, None, :]
    paired_part = matrix[:, :, :ROT].reshape(row_count, head_count, half_rot, 2)
    even_part = paired_part[:, :, :, 0]
    odd_part = paired_part[:, :, :, 1]
    turned = jnp.stack(
        [even_part * cosine - odd_part * sine_value, odd_part * cosine + even_part * sine_value],
        axis=-1,
    )
    return jnp.concatenate([turned.reshape(row_count, head_count, ROT), matrix[:, :, ROT:]], axis=2)


def slot_selector(products, chosen, adapter_id, column_count):
    row_count = products.shape[0]
    selector = (adapter_id[:, None] == chosen[None, :]).astype(jnp.float32)
    reshaped = products.reshape(row_count, chosen.shape[0], column_count)
    return jnp.sum(selector[:, :, None] * reshaped, axis=1)


def widen_rows(values, chosen, adapter_id):
    selector = adapter_id[:, None] == chosen[None, :]
    spread = jnp.where(selector[:, :, None], values[:, None, :], jnp.zeros((), values.dtype))
    return spread.reshape(values.shape[0], chosen.shape[0] * values.shape[1])


def per_device(
    tokens,
    layer_norm_gain,
    layer_norm_bias,
    query_key_weight,
    output_weight,
    up_weight,
    input_bias,
    down_weight,
    output_bias,
    input_adapter_left,
    query_key_value_right,
    up_adapter_right,
    output_adapter_left,
    down_adapter_left,
    output_adapter_right,
    lengths,
    request_adapter,
    slot_adapter,
):
    tok_dev = tokens.shape[0]
    model_width = tokens.shape[1]
    mlp_count = lax.axis_size("mlp")
    tok_grp = tok_dev * mlp_count
    group_first = lax.axis_index("req") * tok_grp
    heads_local = query_key_weight.shape[1]
    hid_local = up_weight.shape[1]
    adapter_ids = slot_adapter.shape[0] * mlp_count
    every_id = lax.iota(jnp.int32, adapter_ids)
    query_key_columns = heads_local * 3 * HEAD_SIZE
    attention_columns = heads_local * HEAD_SIZE
    query_key_rows = query_key_weight.reshape(model_width, query_key_columns)
    normed_rows = normalize(tokens, layer_norm_gain, layer_norm_bias)
    slot_portion = lax.all_gather(normed_rows, "mlp", axis=0, tiled=True)
    grouped = jnp.concatenate(
        [
            rank_product(slot_portion, query_key_rows),
            rank_product(slot_portion, up_weight),
            rank_product(slot_portion, input_adapter_left),
        ],
        axis=1,
    )
    token_index, request, position, adapter_id = token_info(
        lengths, request_adapter, group_first, tok_grp
    )
    rank_part = slot_selector(
        grouped[:, query_key_columns + hid_local :], slot_adapter, adapter_id, 2 * ADAPTER_RANK
    )
    rank_input = lax.psum(rank_part.astype(jnp.bfloat16), "mlp")
    qkv_extra = rank_product(
        widen_rows(rank_input[:, :ADAPTER_RANK], every_id, adapter_id),
        query_key_value_right.reshape(adapter_ids * ADAPTER_RANK, query_key_columns),
    )
    up_delta = rank_product(
        widen_rows(rank_input[:, ADAPTER_RANK:], every_id, adapter_id), up_adapter_right
    )
    projected_rows = (grouped[:, :query_key_columns] + qkv_extra).reshape(
        tok_grp, heads_local, 3 * HEAD_SIZE
    )
    hidden_units = jax.nn.gelu(
        grouped[:, query_key_columns : query_key_columns + hid_local] + up_delta + input_bias,
        approximate=True,
    ).astype(jnp.bfloat16)
    queries = rotate(projected_rows[:, :, :HEAD_SIZE], position).astype(jnp.bfloat16)
    key_rows = (
        rotate(projected_rows[:, :, HEAD_SIZE : 2 * HEAD_SIZE], position)
        .astype(jnp.bfloat16)
        .reshape(tok_grp, attention_columns)
    )
    value_rows = (
        projected_rows[:, :, 2 * HEAD_SIZE :]
        .astype(jnp.bfloat16)
        .reshape(tok_grp, attention_columns)
    )
    paired = jnp.stack([key_rows, value_rows])
    score_scale = HEAD_SIZE ** (-0.5)
    last_row = group_first + tok_grp - 1
    start_state = (
        jnp.full((tok_grp, heads_local), NEGATIVE_FILL, jnp.float32),
        jnp.zeros((tok_grp, heads_local), jnp.float32),
        jnp.zeros((tok_grp, heads_local, HEAD_SIZE), jnp.float32),
    )
    slot_portion = lax.all_gather(paired, "req", axis=1, tiled=True)
    offset = jnp.int32(0)
    amount = slot_portion.shape[1]
    key_index, key_request, key_position, key_adapter = token_info(
        lengths, request_adapter, offset, amount
    )
    useful = jnp.logical_and(offset <= last_row, key_request[amount - 1] >= request[0])

    def attend(current):
        running_top, running_total, running_sum = current
        part_keys = slot_portion[0].reshape(amount, heads_local, HEAD_SIZE)
        part_values = slot_portion[1].reshape(amount, heads_local, HEAD_SIZE)
        scores = (
            jnp.einsum("qhd,khd->qhk", queries, part_keys, preferred_element_type=jnp.float32)
            * score_scale
        )
        allowed = jnp.logical_and(
            key_request[None, :] == request[:, None], key_index[None, :] <= token_index[:, None]
        )[:, None, :]
        masked = jnp.where(allowed, scores, NEGATIVE_FILL)
        new_top = jnp.maximum(running_top, jnp.max(masked, axis=2))
        weights = jnp.where(allowed, jnp.exp(masked - new_top[:, :, None]), 0.0)
        new_total = jnp.sum(weights, axis=2)
        new_sum = jnp.einsum(
            "qhk,khd->qhd",
            weights.astype(jnp.bfloat16),
            part_values,
            preferred_element_type=jnp.float32,
        )
        return (new_top, new_total, new_sum)

    final_state = lax.cond(useful, attend, lambda current: current, start_state)
    attention_output = (
        (final_state[2] / final_state[1][:, :, None])
        .astype(jnp.bfloat16)
        .reshape(tok_grp, attention_columns)
    )
    output_rows = output_weight.reshape(attention_columns, model_width)
    own_ids = lax.axis_index("mlp") * ADP_DEV + lax.iota(jnp.int32, ADP_DEV)
    output_rank_rows = rank_product(
        attention_output, output_adapter_left.reshape(attention_columns, adapter_ids * ADAPTER_RANK)
    )
    down_rank_rows = rank_product(hidden_units, down_adapter_left)
    rank_part_out = jnp.concatenate(
        [
            slot_selector(output_rank_rows, every_id, adapter_id, ADAPTER_RANK),
            slot_selector(down_rank_rows, every_id, adapter_id, ADAPTER_RANK),
        ],
        axis=1,
    )
    rank_output = lax.psum(rank_part_out.astype(jnp.bfloat16), "mlp")
    rank_widened = widen_rows(rank_output, own_ids, adapter_id)
    mixed = lax.psum_scatter(
        (
            rank_product(attention_output, output_rows)
            + (
                rank_product(hidden_units, down_weight)
                + rank_product(rank_widened, output_adapter_right)
            )
        ).astype(jnp.bfloat16),
        "mlp",
        scatter_dimension=0,
        tiled=True,
    ).astype(jnp.float32)
    return (mixed + tokens.astype(jnp.float32) + output_bias).astype(jnp.bfloat16)


def solution(mesh):
    in_specs = (
        P(("req", "mlp"), None),
        P(),
        P(),
        P(None, "mlp", None),
        P("mlp", None, None),
        P(None, "mlp"),
        P("mlp"),
        P("mlp", None),
        P(),
        P(None, "mlp"),
        P(None, "mlp", None),
        P(None, "mlp"),
        P("mlp", None, None),
        P("mlp", None),
        P("mlp", None),
        P(),
        P(),
        P("mlp"),
    )
    out_specs = P(("req", "mlp"), None)
    return jax.shard_map(
        per_device, mesh=mesh, in_specs=in_specs, out_specs=out_specs, check_vma=False
    )
```

profile of v0, /device:TPU:0, one launch (start us, length us, event | category | flops | bytes accessed | tf_op | source)
XLA Modules:
  0.0 493.8 jit_solution(12925493245137740278)
XLA Ops:
  6.5 1.4 convert_reduce_fusion.1
  7.9 1.3 fusion.35
  9.3 2.1 fusion.38
  11.4 0.0 all-gather.3.cloned.1.call-update
  11.4 0.0 all-reduce.4.cloned.1.call-start
  11.5 0.7 pad_bitcast_fusion
  12.2 0.3 reduce-window.9
  12.5 0.1 slice.64
  12.6 0.1 slice_reduce_fusion
  12.7 0.1 add_bitcast_fusion.1
  12.8 0.7 slice_subtract_fusion
  13.5 0.3 fusion.34
  13.8 6.2 %gather_fusion = s32[1024]{0:T(1024)S(1)} fusion(s32[257]{0:T(512)} %param.36, s32[1024]{0:T(1024)S(1)} %maximum_clamp_fusion), kind=kCustom, calls=%fused_computation | custom fusion | bytes 12288 | tf_op jit(solution)/shard_map/jit(_take)/gather | solution.py:34
  20.0 0.1 broadcast_compare_fusion
  20.1 0.8 fusion.60
  20.8 64.1 %all-gather.3.cloned.1.call-done = bf16[1024,4096]{1,0:T(8,128)(2,1)} async-done(((bf16[64,4096]{1,0:T(8,128)(2,1)}), bf16[1024,4096]{1,0:T(8,128)(2,1)}) %all-gather.3.cloned.1.call-update) | async-done | bytes 8388624 | tf_op jit(solution)/shard_map/all_gather | solution.py:102
  84.9 6.3 %fusion.67 = f32[1024,128]{0,1:T(8,128)S(1)} fusion(bf16[1024,4096]{1,0:T(8,128)(2,1)} %all-gather.3.cloned.1.call-done, bf16[4096,128]{1,0:T(8,128)(2,1)S(1)} %copy-done.2), kind=kOutput, calls=%fused_computation.113 | convolution fusion | flops 1073741824 | bytes 9961472 | tf_op jit(solution)/shard_map/dot_general | solution.py:16
  91.2 0.7 multiply_reduce_fusion.1
  91.9 0.0 all-reduce.4.cloned.1.call-update
  91.9 0.0 all-gather.5.cloned.1.call-start
  91.9 0.6 multiply_exponential_fusion
  92.5 80.1 %all-reduce.4.cloned.1.call-done = bf16[1024,32]{0,1:T(8,128)(2,1)} async-done(((bf16[1024,32]{0,1:T(8,128)(2,1)}), bf16[1024,32]{0,1:T(8,128)(2,1)}) %all-reduce.4.cloned.1.call-update) | async-done | bytes 65552 | tf_op jit(solution)/shard_map/psum | solution.py:117
  172.6 0.8 fusion.65
  173.4 1.8 broadcast_select_fusion
  175.2 3.3 fusion.29
  178.5 11.0 %fusion.66 = (bf16[1024,1,768]{0,2,1:T(8,128)(2,1)S(1)}, f32[1024,1,768]{0,2,1:T(8,128)S(1)}) fusion(f32[1024,768]{0,1:T(8,128)S(1)} %fusion.29, bf16[1024,4096]{1,0:T(8,128)(2,1)} %all-gather.3.cloned.1.call-done, bf16[4096,1,768]{2,0,1:T(8,128)(2,1)} %param.23), kind=kOutput, calls=%fused_computation.112 | convolution fusion | flops 6444023808 | bytes 22544384 | tf_op jit(solution)/shard_map/dot_general | solution.py:16
  189.5 0.1 fusion.62
  189.6 0.8 fusion.61
  190.4 2.0 reshape.569
  192.4 1.6 fusion.63
  194.0 2.0 reshape.568
  196.0 1.0 fusion.64
  197.0 2.2 fusion.57
  199.2 0.8 copy.41
  200.0 1.0 concatenate.35
  200.9 1.1 pad_maximum_fusion
  202.1 0.2 all-reduce.6.cloned.1.call-start
  202.3 0.6 slice.68
  202.9 1.3 convert_reduce_fusion
  204.2 0.6 slice.84
  206.1 2.0 copy.47
  208.2 11.3 %fusion.68 = f32[1024,512]{1,0:T(8,128)} fusion(bf16[1024,4096]{1,0:T(8,128)(2,1)} %all-gather.3.cloned.1.call-done, bf16[4096,512]{1,0:T(8,128)(2,1)} %param.25), kind=kOutput, calls=%fused_computation.114 | convolution fusion | flops 4294967296 | bytes 14680064 | tf_op jit(solution)/shard_map/dot_general | solution.py:16
  219.5 0.1 copy.44
  219.7 0.1 concatenate.38
  219.7 0.8 pad_maximum_fusion.1
  220.6 4.5 fusion.24
  225.1 1.3 fusion.70
  226.5 2.4 fusion.16
  228.9 8.3 %fusion.69 = f32[1024,4096]{1,0:T(8,128)} fusion(bf16[1024,512]{1,0:T(8,128)(2,1)S(1)} %fusion.24, bf16[512,4096]{1,0:T(8,128)(2,1)S(1)} %copy-done.9), kind=kOutput, calls=%fused_computation.115 | convolution fusion | flops 4294967296 | bytes 22020096 | tf_op jit(solution)/shard_map/dot_general | solution.py:16
  237.2 14.0 %all-gather.5.cloned.1.call-done = bf16[2,8192,256]{1,2,0:T(8,128)(2,1)} async-done(((bf16[2,1024,256]{1,2,0:T(8,128)(2,1)}), bf16[2,8192,256]{1,2,0:T(8,128)(2,1)}) %all-gather.5.cloned.1.call-update) | async-done | bytes 8388624 | tf_op jit(solution)/shard_map/all_gather | solution.py:151
  251.2 49.0 %conditional.1 = (f32[1024,1]{0,1:T(1,128)S(1)}, f32[1024,1,256]{2,0,1:T(8,128)S(1)}) conditional(s32[]{:T(128)} %convert_element_type.83, () %tuple.13, (s32[8192]{0:T(1024)S(1)}, s32[1024]{0:T(1024)S(1)}, s32[8192]{0:T(1024)S(1)}, s32[]{:T(128)}, s32[1024]{0:T(1024)S(1)}, /*index=5*/bf16[2,8192,256]{1,2,0:T(8,128)(2,1)}, ...), branch_computations={%region_9.10_spmd, %region_10.13_spmd} | conditional | flops 8774483968 | bytes 129753136 | solution.py:182
  251.2 12.0 %copy.45 = bf16[2,8192,256]{2,1,0:T(8,128)(2,1)} copy(bf16[2,8192,256]{1,2,0:T(8,128)(2,1)} %get-tuple-element.65) | data formatting | bytes 16777216 | tf_op jit(solution)/shard_map
  263.2 10.0 %fusion = (f32[1024]{0:T(1024)S(1)}, f32[8192,1024]{1,0:T(8,128)S(1)}) fusion(s32[1024]{0:T(1024)S(1)} %broadcast_add_fusion, s32[1024]{0:T(1024)S(1)} %get-tuple-element.22, s32[8192]{0:T(1024)S(1)} %get-tuple-element.23, s32[8192]{0:T(1024)S(1)} %get-tuple-element.21, bf16[1024,1,256]{0,2,1:T(8,128)(2,1)S(1)} %copy-done.4, bf16[2,8192,256]{2,1,0:T(8,128)(2,1)} %copy.45), kind=kOutput, calls=%fused_computation.4 | convolution fusion | flops 4345297920 | bytes 38350848 | tf_op jit(solution)/shard_map/cond/branch_1_fun/qhd,khd->qhk/dot_general | solution.py:164
  273.2 14.2 %fusion.7 = f32[1024,1,256]{2,0,1:T(8,128)S(1)} fusion(bf16[2,8192,256]{2,1,0:T(8,128)(2,1)} %copy.45, f32[8192,1024]{1,0:T(8,128)S(1)} %get-tuple-element.70, f32[1024]{0:T(1024)S(1)} %broadcast_maximum_fusion, s32[1024]{0:T(1024)S(1)} %broadcast_add_fusion, s32[1024]{0:T(1024)S(1)} %get-tuple-element.22, s32[8192]{0:T(1024)S(1)} %get-tuple-element.23, ...), kind=kOutput, calls=%fused_computation.12 | convolution fusion | flops 4362076160 | bytes 38875136 | tf_op jit(solution)/shard_map/cond/branch_1_fun/qhk,khd->qhd/dot_general | solution.py:174
  287.4 12.8 %fusion.2 = f32[1024]{0:T(1024)S(1)} fusion(f32[8192,1024]{1,0:T(8,128)S(1)} %get-tuple-element.70, f32[1024]{0:T(1024)S(1)} %broadcast_maximum_fusion, s32[1024]{0:T(1024)S(1)} %broadcast_add_fusion, s32[1024]{0:T(1024)S(1)} %get-tuple-element.22, s32[8192]{0:T(1024)S(1)} %get-tuple-element.23, s32[8192]{0:T(1024)S(1)} %get-tuple-element.21), kind=kLoop, calls=%fused_computation.6 | loop fusion | flops 67107840 | bytes 33636352 | tf_op jit(solution)/shard_map/cond/branch_1_fun/reduce_sum | solution.py:173
  300.2 1.9 multiply_reduce_fusion
  302.2 0.6 pad_maximum_fusion.4
  302.8 0.0 reduce-scatter.2.cloned.1.call-start
  302.9 8.1 %fusion.25 = f32[1024,4096]{1,0:T(8,128)} fusion(bf16[1,256,4096]{2,1,0:T(8,128)(2,1)S(1)} %copy-done, f32[1024,1,256]{2,0,1:T(8,128)S(1)} %get-tuple-element.30, f32[1024]{0:T(1024)S(1)} %bitcast.116), kind=kOutput, calls=%fused_computation.37 | convolution fusion | flops 2148007936 | bytes 19927040 | tf_op jit(solution)/shard_map/dot_general | solution.py:16
  311.0 73.2 %all-reduce.6.cloned.1.call-done = bf16[1024,32]{0,1:T(8,128)(2,1)} async-done(((bf16[1024,32]{0,1:T(8,128)(2,1)}), bf16[1024,32]{0,1:T(8,128)(2,1)}) %all-reduce.6.cloned.1.call-update) | async-done | bytes 65552 | tf_op jit(solution)/shard_map/psum | solution.py:201
  384.2 0.9 broadcast_select_fusion.2
  385.0 15.6 %add_convert_fusion = bf16[1024,4096]{1,0:T(8,128)(2,1)} fusion(f32[1024,4096]{1,0:T(8,128)} %fusion.25, f32[1024,4096]{1,0:T(8,128)} %fusion.69, bf16[1024,128]{0,1:T(8,128)(2,1)S(1)} %bitcast.112, bf16[128,4096]{1,0:T(8,128)(2,1)} %param.34), kind=kOutput, calls=%fused_computation.19 | convolution fusion | flops 1086324736 | bytes 43253760 | tf_op jit(solution)/shard_map/dot_general | solution.py:16
  400.7 84.6 %reduce-scatter.2.cloned.1.call-done = bf16[64,4096]{1,0:T(8,128)(2,1)} async-done(((bf16[1024,4096]{1,0:T(8,128)(2,1)}), bf16[64,4096]{1,0:T(8,128)(2,1)}) %reduce-scatter.2.cloned.1.call-update) | async-done | bytes 524304 | tf_op jit(solution)/shard_map/reduce_scatter | solution.py:203
  485.3 2.0 fusion.40
  (43 shorter events, 0.3 us)
Async XLA Ops:
  6.5 296.3 %copy-start = (bf16[1,256,4096]{2,1,0:T(8,128)(2,1)S(1)}, bf16[1,256,4096]{2,1,0:T(8,128)(2,1)}, u32[]{:S(2)}) copy-start(bf16[1,256,4096]{2,1,0:T(8,128)(2,1)} %param.24) | copy-start | bytes 6291460
  6.5 13.5 %copy-start.8 = (s32[4]{0:T(128)S(1)}, s32[4]{0:T(128)}, u32[]{:S(2)}) copy-start(s32[4]{0:T(128)} %param.37) | copy-start | bytes 52
  6.5 78.4 %copy-start.2 = (bf16[4096,128]{1,0:T(8,128)(2,1)S(1)}, bf16[4096,128]{1,0:T(8,128)(2,1)}, u32[]{:S(2)}) copy-start(bf16[4096,128]{1,0:T(8,128)(2,1)} %param.29) | copy-start | bytes 3145732
  6.5 78.4 %all-gather.3.cloned.1.call-start = ((), (), s32[]{:S(2)}) async-start(), calls=%async_computation.1 | async-start | bytes 8912896 | tf_op jit(solution)/shard_map/all_gather | solution.py:102
  11.4 161.2 %all-reduce.4.cloned.1.call-start = ((), (), s32[]{:S(2)}) async-start(), calls=%async_computation.2 | async-start | bytes 131072 | tf_op jit(solution)/shard_map/psum | solution.py:117
  91.9 159.3 %all-gather.5.cloned.1.call-start = ((), (), s32[]{:S(2)}) async-start(), calls=%async_computation.3 | async-start | bytes 9437184 | tf_op jit(solution)/shard_map/all_gather | solution.py:151
  202.1 182.1 %all-reduce.6.cloned.1.call-start = ((), (), s32[]{:S(2)}) async-start(), calls=%async_computation.4 | async-start | bytes 131072 | tf_op jit(solution)/shard_map/psum | solution.py:201
  208.2 11.3 %copy-start.5 = (bf16[1024,1,32,1]{0,2,3,1:T(8,128)(2,1)S(1)}, bf16[1024,1,32,1]{0,2,3,1:T(8,128)(2,1)}, u32[]{:S(2)}) copy-start(bf16[1024,1,32,1]{0,2,3,1:T(8,128)(2,1)} %get-tuple-element.75) | copy-start | bytes 196612
  208.2 11.3 %copy-start.6 = (bf16[1024,1,32,1]{0,2,3,1:T(8,128)(2,1)S(1)}, bf16[1024,1,32,1]{0,2,3,1:T(8,128)(2,1)}, u32[]{:S(2)}) copy-start(bf16[1024,1,32,1]{0,2,3,1:T(8,128)(2,1)} %get-tuple-element.76) | copy-start | bytes 196612
  208.2 12.4 %copy-start.11 = (f32[512]{0:T(512)S(1)}, f32[512]{0:T(512)}, u32[]{:S(2)}) copy-start(f32[512]{0:T(512)} %param.26) | copy-start | bytes 6148
  220.6 4.6 copy-start.10
  225.1 1.4 copy-start.3
  225.1 3.8 copy-start.9
  251.2 12.0 %copy-start.4 = (bf16[1024,1,256]{0,2,1:T(8,128)(2,1)S(1)}, bf16[1024,1,256]{0,2,1:T(8,128)(2,1)}, u32[]{:S(2)}) copy-start(bf16[1024,1,256]{0,2,1:T(8,128)(2,1)} %get-tuple-element.66) | copy-start | bytes 1572868 | tf_op jit(solution)/shard_map/cond
  302.8 182.5 %reduce-scatter.2.cloned.1.call-start = ((), (), s32[]{:S(2)}) async-start(), calls=%async_computation.5 | async-start | bytes 8912896 | tf_op jit(solution)/shard_map/reduce_scatter | solution.py:203
  400.6 84.7 %copy-start.1 = (bf16[64,4096]{1,0:T(8,128)(2,1)S(1)}, bf16[64,4096]{1,0:T(8,128)(2,1)}, u32[]{:S(2)}) copy-start(bf16[64,4096]{1,0:T(8,128)(2,1)} %param.20) | copy-start | bytes 1572868
  400.6 84.7 %copy-start.7 = (f32[4096]{0:T(1024)S(1)}, f32[4096]{0:T(1024)}, u32[]{:S(2)}) copy-start(f32[4096]{0:T(1024)} %param.28) | copy-start | bytes 49156
Sparse Core Ops, SparseCore 0:
  11.5 73.3 all-gather.2
  92.0 80.5 all-reduce.3
  202.2 48.9 all-gather.4
  302.9 81.1 all-reduce.5
  400.8 84.4 reduce-scatter.1
where the time goes:
time: 495 us; the launch traced here: 494 us
  waiting for transfers between devices  316 us (64%)
  matrix products  95.9 us (19%)
  other arithmetic  34.2 us (7%)
  local copies, waits for them, and re-layouts  32.5 us (7%)
  between operations  14.7 us (3%)
    reduce_scatter x1, waiting for transfers between devices, per_device(): lax.psum_scatter((rank_product(attention_output, output_rows) + (rank_pro...  84.6 us
    psum x1, waiting for transfers between devices, per_device(): rank_input = lax.psum(rank_part.astype(jnp.bfloat16), 'mlp')  80.1 us
    psum x1, waiting for transfers between devices, per_device(): rank_output = lax.psum(rank_part_out.astype(jnp.bfloat16), 'mlp')  73.2 us
    dot_general x10, matrix products, rank_product(): return jnp.dot(left_side, right_side, preferred_element_type=jnp.float32)  71.7 us
    all_gather x1, waiting for transfers between devices, per_device(): slot_portion = lax.all_gather(normed_rows, 'mlp', axis=0, tiled=True)  64.1 us
    dot_general x1, matrix products, attend(): jnp.einsum('qhk,khd->qhd', weights.astype(jnp.bfloat16), part_values, pre...  14.2 us
    all_gather x1, waiting for transfers between devices, per_device(): slot_portion = lax.all_gather(paired, 'req', axis=1, tiled=True)  14 us
    reduce_sum x1, other arithmetic, attend(): new_total = jnp.sum(weights, axis=2)  12.8 us
  transfers between devices with their start and end apart: 5, of which 5 were waited for; matrix products, arithmetic and copies ran while one was open for 10% of the time, Pallas kernels for 0%

commit v1 on v0

--- a/solution.py
+++ b/solution.py
@@ -99,7 +99,8 @@
     attention_columns = heads_local * HEAD_SIZE
     query_key_rows = query_key_weight.reshape(model_width, query_key_columns)
     normed_rows = normalize(tokens, layer_norm_gain, layer_norm_bias)
-    slot_portion = lax.all_gather(normed_rows, "mlp", axis=0, tiled=True)
+    outgoing = jnp.stack([normed_rows] * lax.axis_size("mlp"))
+    slot_portion = jnp.concatenate(lax.all_to_all(outgoing, "mlp", 0, 0), axis=0)
     grouped = jnp.concatenate(
         [
             rank_product(slot_portion, query_key_rows),

time: 495 us -> 558 us (1.13)
  waiting for transfers between devices: 316 us -> 366 us
  starting transfers between devices: 0.35 us -> 8.88 us
  local copies, waits for them, and re-layouts: 32.5 us -> 38.1 us
    all_to_all x0 -> x1, waiting for transfers between devices: none -> 114 us  [per_device(): lax.all_to_all(outgoing, 'mlp', 0, 0)]
    all_gather x1 -> x0, waiting for transfers between devices: 64.1 us -> none  [per_device(): slot_portion = lax.all_gather(normed_rows, 'mlp', axis=0, tiled=True)]
    all_to_all x0 -> x1, starting transfers between devices: none -> 8.31 us  [per_device(): lax.all_to_all(outgoing, 'mlp', 0, 0)]
    another operation x2 -> x3, local copies, waits for them, and re-layouts: 12.1 us -> 16.4 us
  transfers between devices with their start and end apart: 5 -> 5, of which waited for: 5 -> 5; matrix products, arithmetic and copies ran while one was open for 10% -> 9% of each run, Pallas kernels for 0% -> 0%
where the time goes in v1:
time: 558 us; the launch traced here: 557 us
  waiting for transfers between devices  366 us (66%)
  matrix products  96.8 us (17%)
  local copies, waits for them, and re-layouts  38.1 us (7%)
  other arithmetic  32.1 us (6%)
  between operations  14.7 us (3%)
  starting transfers between devices  8.88 us (2%)
    all_to_all x1, waiting for transfers between devices, per_device(): lax.all_to_all(outgoing, 'mlp', 0, 0)  114 us
    reduce_scatter x1, waiting for transfers between devices, per_device(): lax.psum_scatter((rank_product(attention_output, output_rows) + (rank_pro...  84.6 us
    psum x1, waiting for transfers between devices, per_device(): rank_input = lax.psum(rank_part.astype(jnp.bfloat16), 'mlp')  80.3 us
    psum x1, waiting for transfers between devices, per_device(): rank_output = lax.psum(rank_part_out.astype(jnp.bfloat16), 'mlp')  73.2 us
    dot_general x10, matrix products, rank_product(): return jnp.dot(left_side, right_side, preferred_element_type=jnp.float32)  72.6 us
    dot_general x1, matrix products, attend(): jnp.einsum('qhk,khd->qhd', weights.astype(jnp.bfloat16), part_values, pre...  14.2 us
    all_gather x1, waiting for transfers between devices, per_device(): slot_portion = lax.all_gather(paired, 'req', axis=1, tiled=True)  13.9 us
    reduce_sum x1, other arithmetic, attend(): new_total = jnp.sum(weights, axis=2)  12.8 us
  transfers between devices with their start and end apart: 5, of which 5 were waited for; matrix products, arithmetic and copies ran while one was open for 9% of the time, Pallas kernels for 0%

profile of v1, /device:TPU:0, one launch (start us, length us, event | category | flops | bytes accessed | tf_op | source)
XLA Modules:
  0.0 556.6 jit_solution(14011771622900082117)
XLA Ops:
  6.5 1.4 convert_reduce_fusion.1
  7.9 1.3 fusion.36
  9.3 1.3 fusion.39
  10.6 4.3 stack.10
  14.9 8.3 %all-to-all-start = ((bf16[16,64,4096]{2,1,0:T(8,128)(2,1)}), bf16[16,64,4096]{2,1,0:T(8,128)(2,1)}, u32[]{:S(2)}, u32[]{:S(2)}) async-start(bf16[16,64,4096]{2,1,0:T(8,128)(2,1)} %stack.10), calls=%async_computation | async-start | bytes 16777216 | tf_op jit(solution)/shard_map/all_to_all | solution.py:103
  23.2 0.0 all-reduce.4.cloned.1.call-start
  23.3 0.3 reduce-window.9
  23.6 0.1 slice.64
  23.7 1.3 copy.43
  25.0 0.1 slice_reduce_fusion
  25.1 0.1 add_bitcast_fusion.1
  25.2 0.3 fusion.35
  25.5 6.9 %gather_fusion = s32[1024]{0:T(1024)S(1)} fusion(s32[257]{0:T(512)S(1)} %copy-done.1, s32[1024]{0:T(1024)S(1)} %maximum_clamp_fusion), kind=kCustom, calls=%fused_computation | custom fusion | bytes 12288 | tf_op jit(solution)/shard_map/jit(_take)/gather | solution.py:34
  32.4 0.1 broadcast_compare_fusion
  32.5 0.8 fusion.61
  33.3 113.9 %all-to-all-done = bf16[16,64,4096]{2,1,0:T(8,128)(2,1)} async-done(((bf16[16,64,4096]{2,1,0:T(8,128)(2,1)}), bf16[16,64,4096]{2,1,0:T(8,128)(2,1)}, u32[]{:S(2)}, u32[]{:S(2)}) %all-to-all-start) | async-done | bytes 8388640 | tf_op jit(solution)/shard_map/all_to_all | solution.py:103
  147.2 7.2 %fusion.33 = bf16[1024,32]{0,1:T(8,128)(2,1)} fusion(bf16[1024,4096,1]{1,0,2:T(8,128)(2,1)} %bitcast.15, bf16[4,32,4096]{2,1,0:T(8,128)(2,1)} %bitcast.117, f32[1024,4]{0,1:T(4,128)S(1)} %get-tuple-element.92), kind=kOutput, calls=%fused_computation.51 | convolution fusion | flops 1073971200 | bytes 9519104 | tf_op jit(solution)/shard_map/dot_general | solution.py:16
  154.4 0.0 all-reduce.4.cloned.1.call-update
  154.4 0.2 all-gather.2.cloned.1.call-start
  154.6 0.6 multiply_exponential_fusion
  155.2 80.3 %all-reduce.4.cloned.1.call-done = bf16[1024,32]{0,1:T(8,128)(2,1)} async-done(((bf16[1024,32]{0,1:T(8,128)(2,1)}), bf16[1024,32]{0,1:T(8,128)(2,1)}) %all-reduce.4.cloned.1.call-update) | async-done | bytes 65552 | tf_op jit(solution)/shard_map/psum | solution.py:118
  235.5 0.8 fusion.66
  236.3 1.8 broadcast_select_fusion
  238.0 3.3 fusion.29
  241.3 11.0 %fusion.67 = (bf16[1024,1,768]{0,2,1:T(8,128)(2,1)S(1)}, f32[1024,1,768]{0,2,1:T(8,128)S(1)}) fusion(f32[1024,768]{0,1:T(8,128)S(1)} %fusion.29, bf16[1024,4096]{1,0:T(8,128)(2,1)} %bitcast.13, bf16[4096,1,768]{2,0,1:T(8,128)(2,1)} %param.23), kind=kOutput, calls=%fused_computation.113 | convolution fusion | flops 6444023808 | bytes 22544384 | tf_op jit(solution)/shard_map/dot_general | solution.py:16
  252.4 0.1 fusion.63
  252.5 0.8 fusion.62
  253.3 2.0 reshape.573
  255.3 1.6 fusion.64
  256.9 2.0 reshape.572
  258.9 1.0 fusion.65
  259.9 2.2 fusion.58
  262.1 0.8 copy.46
  262.8 1.0 concatenate.35
  263.8 1.1 pad_maximum_fusion
  264.9 0.0 all-gather.2.cloned.1.call-update
  265.0 0.3 all-reduce.6.cloned.1.call-start
  265.2 0.6 slice.68
  265.8 1.3 convert_reduce_fusion
  267.1 0.6 slice.84
  269.0 2.0 copy.52
  271.1 11.4 %fusion.68 = f32[1024,512]{1,0:T(8,128)} fusion(bf16[1024,4096]{1,0:T(8,128)(2,1)} %bitcast.13, bf16[4096,512]{1,0:T(8,128)(2,1)} %param.25), kind=kOutput, calls=%fused_computation.114 | convolution fusion | flops 4294967296 | bytes 14680064 | tf_op jit(solution)/shard_map/dot_general | solution.py:16
  282.5 0.1 copy.49
  282.6 0.1 concatenate.38
  282.7 0.8 pad_maximum_fusion.1
  283.5 4.5 fusion.24
  288.1 1.3 fusion.70
  289.4 2.4 fusion.16
  291.8 8.3 %fusion.69 = f32[1024,4096]{1,0:T(8,128)} fusion(bf16[1024,512]{1,0:T(8,128)(2,1)S(1)} %fusion.24, bf16[512,4096]{1,0:T(8,128)(2,1)S(1)} %copy-done.11), kind=kOutput, calls=%fused_computation.115 | convolution fusion | flops 4294967296 | bytes 22020096 | tf_op jit(solution)/shard_map/dot_general | solution.py:16
  300.1 13.9 %all-gather.2.cloned.1.call-done = bf16[2,8192,256]{1,2,0:T(8,128)(2,1)} async-done(((bf16[2,1024,256]{1,2,0:T(8,128)(2,1)}), bf16[2,8192,256]{1,2,0:T(8,128)(2,1)}) %all-gather.2.cloned.1.call-update) | async-done | bytes 8388624 | tf_op jit(solution)/shard_map/all_gather | solution.py:152
  314.1 49.0 %conditional.1 = (f32[1024,1]{0,1:T(1,128)S(1)}, f32[1024,1,256]{2,0,1:T(8,128)S(1)}) conditional(s32[]{:T(128)} %convert_element_type.83, () %tuple.13, (s32[8192]{0:T(1024)S(1)}, s32[1024]{0:T(1024)S(1)}, s32[8192]{0:T(1024)S(1)}, s32[]{:T(128)}, s32[1024]{0:T(1024)S(1)}, /*index=5*/bf16[2,8192,256]{1,2,0:T(8,128)(2,1)}, ...), branch_computations={%region_9.10_spmd, %region_10.13_spmd} | conditional | flops 8774483968 | bytes 129753136 | solution.py:183
  314.1 12.0 %copy.50 = bf16[2,8192,256]{2,1,0:T(8,128)(2,1)} copy(bf16[2,8192,256]{1,2,0:T(8,128)(2,1)} %get-tuple-element.65) | data formatting | bytes 16777216 | tf_op jit(solution)/shard_map
  326.1 10.0 %fusion = (f32[1024]{0:T(1024)S(1)}, f32[8192,1024]{1,0:T(8,128)S(1)}) fusion(s32[1024]{0:T(1024)S(1)} %broadcast_add_fusion, s32[1024]{0:T(1024)S(1)} %get-tuple-element.22, s32[8192]{0:T(1024)S(1)} %get-tuple-element.23, s32[8192]{0:T(1024)S(1)} %get-tuple-element.21, bf16[1024,1,256]{0,2,1:T(8,128)(2,1)S(1)} %copy-done.5, bf16[2,8192,256]{2,1,0:T(8,128)(2,1)} %copy.50), kind=kOutput, calls=%fused_computation.4 | convolution fusion | flops 4345297920 | bytes 38350848 | tf_op jit(solution)/shard_map/cond/branch_1_fun/qhd,khd->qhk/dot_general | solution.py:165
  336.1 14.2 %fusion.7 = f32[1024,1,256]{2,0,1:T(8,128)S(1)} fusion(bf16[2,8192,256]{2,1,0:T(8,128)(2,1)} %copy.50, f32[8192,1024]{1,0:T(8,128)S(1)} %get-tuple-element.70, f32[1024]{0:T(1024)S(1)} %broadcast_maximum_fusion, s32[1024]{0:T(1024)S(1)} %broadcast_add_fusion, s32[1024]{0:T(1024)S(1)} %get-tuple-element.22, s32[8192]{0:T(1024)S(1)} %get-tuple-element.23, ...), kind=kOutput, calls=%fused_computation.12 | convolution fusion | flops 4362076160 | bytes 38875136 | tf_op jit(solution)/shard_map/cond/branch_1_fun/qhk,khd->qhd/dot_general | solution.py:175
  350.3 12.8 %fusion.2 = f32[1024]{0:T(1024)S(1)} fusion(f32[8192,1024]{1,0:T(8,128)S(1)} %get-tuple-element.70, f32[1024]{0:T(1024)S(1)} %broadcast_maximum_fusion, s32[1024]{0:T(1024)S(1)} %broadcast_add_fusion, s32[1024]{0:T(1024)S(1)} %get-tuple-element.22, s32[8192]{0:T(1024)S(1)} %get-tuple-element.23, s32[8192]{0:T(1024)S(1)} %get-tuple-element.21), kind=kLoop, calls=%fused_computation.6 | loop fusion | flops 67107840 | bytes 33636352 | tf_op jit(solution)/shard_map/cond/branch_1_fun/reduce_sum | solution.py:174
  363.1 1.9 multiply_reduce_fusion
  365.0 0.6 pad_maximum_fusion.4
  365.7 0.0 reduce-scatter.2.cloned.1.call-start
  365.7 8.1 %fusion.25 = f32[1024,4096]{1,0:T(8,128)} fusion(bf16[1,256,4096]{2,1,0:T(8,128)(2,1)S(1)} %copy-done, f32[1024,1,256]{2,0,1:T(8,128)S(1)} %get-tuple-element.30, f32[1024]{0:T(1024)S(1)} %bitcast.121), kind=kOutput, calls=%fused_computation.37 | convolution fusion | flops 2148007936 | bytes 19927040 | tf_op jit(solution)/shard_map/dot_general | solution.py:16
  373.8 73.2 %all-reduce.6.cloned.1.call-done = bf16[1024,32]{0,1:T(8,128)(2,1)} async-done(((bf16[1024,32]{0,1:T(8,128)(2,1)}), bf16[1024,32]{0,1:T(8,128)(2,1)}) %all-reduce.6.cloned.1.call-update) | async-done | bytes 65552 | tf_op jit(solution)/shard_map/psum | solution.py:202
  447.0 0.9 broadcast_select_fusion.2
  447.9 15.6 %add_convert_fusion = bf16[1024,4096]{1,0:T(8,128)(2,1)} fusion(f32[1024,4096]{1,0:T(8,128)} %fusion.25, f32[1024,4096]{1,0:T(8,128)} %fusion.69, bf16[1024,128]{0,1:T(8,128)(2,1)S(1)} %bitcast.116, bf16[128,4096]{1,0:T(8,128)(2,1)} %param.34), kind=kOutput, calls=%fused_computation.19 | convolution fusion | flops 1086324736 | bytes 43253760 | tf_op jit(solution)/shard_map/dot_general | solution.py:16
  463.5 84.6 %reduce-scatter.2.cloned.1.call-done = bf16[64,4096]{1,0:T(8,128)(2,1)} async-done(((bf16[1024,4096]{1,0:T(8,128)(2,1)}), bf16[64,4096]{1,0:T(8,128)(2,1)}) %reduce-scatter.2.cloned.1.call-update) | async-done | bytes 524304 | tf_op jit(solution)/shard_map/reduce_scatter | solution.py:204
  548.1 2.0 fusion.41
  (47 shorter events, 0.3 us)
Async XLA Ops:
  6.5 359.2 %copy-start = (bf16[1,256,4096]{2,1,0:T(8,128)(2,1)S(1)}, bf16[1,256,4096]{2,1,0:T(8,128)(2,1)}, u32[]{:S(2)}) copy-start(bf16[1,256,4096]{2,1,0:T(8,128)(2,1)} %param.24) | copy-start | bytes 6291460
  14.9 8.4 %copy-start.9 = (s32[257]{0:T(512)S(1)}, s32[257]{0:T(512)}, u32[]{:S(2)}) copy-start(s32[257]{0:T(512)} %param.35) | copy-start | bytes 3088
  14.9 8.8 %copy-start.4 = (bf16[4096,128]{1,0:T(8,128)(2,1)S(1)}, bf16[4096,128]{1,0:T(8,128)(2,1)}, u32[]{:S(2)}) copy-start(bf16[4096,128]{1,0:T(8,128)(2,1)} %param.29) | copy-start | bytes 3145732
  14.9 10.7 %copy-start.1 = (s32[257]{0:T(512)S(1)}, s32[257]{0:T(512)}, u32[]{:S(2)}) copy-start(s32[257]{0:T(512)} %param.36) | copy-start | bytes 3088
  14.9 132.3 %all-to-all-start = ((bf16[16,64,4096]{2,1,0:T(8,128)(2,1)}), bf16[16,64,4096]{2,1,0:T(8,128)(2,1)}, u32[]{:S(2)}, u32[]{:S(2)}) async-start(bf16[16,64,4096]{2,1,0:T(8,128)(2,1)} %stack.10), calls=%async_computation | async-start | bytes 16777216 | tf_op jit(solution)/shard_map/all_to_all | solution.py:103
  23.2 9.3 %copy-start.10 = (s32[4]{0:T(128)S(1)}, s32[4]{0:T(128)}, u32[]{:S(2)}) copy-start(s32[4]{0:T(128)} %param.37) | copy-start | bytes 52
  23.2 212.3 %all-reduce.4.cloned.1.call-start = ((), (), s32[]{:S(2)}) async-start(), calls=%async_computation.2 | async-start | bytes 131072 | tf_op jit(solution)/shard_map/psum | solution.py:118
  154.4 159.7 %all-gather.2.cloned.1.call-start = ((), (), s32[]{:S(2)}) async-start(), calls=%async_computation.3 | async-start | bytes 9437184 | tf_op jit(solution)/shard_map/all_gather | solution.py:152
  265.0 182.1 %all-reduce.6.cloned.1.call-start = ((), (), s32[]{:S(2)}) async-start(), calls=%async_computation.4 | async-start | bytes 131072 | tf_op jit(solution)/shard_map/psum | solution.py:202
  271.1 11.4 %copy-start.6 = (bf16[1024,1,32,1]{0,2,3,1:T(8,128)(2,1)S(1)}, bf16[1024,1,32,1]{0,2,3,1:T(8,128)(2,1)}, u32[]{:S(2)}) copy-start(bf16[1024,1,32,1]{0,2,3,1:T(8,128)(2,1)} %get-tuple-element.75) | copy-start | bytes 196612
  271.1 11.4 %copy-start.7 = (bf16[1024,1,32,1]{0,2,3,1:T(8,128)(2,1)S(1)}, bf16[1024,1,32,1]{0,2,3,1:T(8,128)(2,1)}, u32[]{:S(2)}) copy-start(bf16[1024,1,32,1]{0,2,3,1:T(8,128)(2,1)} %get-tuple-element.76) | copy-start | bytes 196612
  271.1 12.4 %copy-start.13 = (f32[512]{0:T(512)S(1)}, f32[512]{0:T(512)}, u32[]{:S(2)}) copy-start(f32[512]{0:T(512)} %param.26) | copy-start | bytes 6148
  283.5 4.6 copy-start.12
  288.1 1.4 copy-start.3
  288.1 3.8 copy-start.11
  314.1 12.0 %copy-start.5 = (bf16[1024,1,256]{0,2,1:T(8,128)(2,1)S(1)}, bf16[1024,1,256]{0,2,1:T(8,128)(2,1)}, u32[]{:S(2)}) copy-start(bf16[1024,1,256]{0,2,1:T(8,128)(2,1)} %get-tuple-element.66) | copy-start | bytes 1572868 | tf_op jit(solution)/shard_map/cond
  365.7 182.4 %reduce-scatter.2.cloned.1.call-start = ((), (), s32[]{:S(2)}) async-start(), calls=%async_computation.5 | async-start | bytes 8912896 | tf_op jit(solution)/shard_map/reduce_scatter | solution.py:204
  463.5 84.6 %copy-start.2 = (bf16[64,4096]{1,0:T(8,128)(2,1)S(1)}, bf16[64,4096]{1,0:T(8,128)(2,1)}, u32[]{:S(2)}) copy-start(bf16[64,4096]{1,0:T(8,128)(2,1)} %param.20) | copy-start | bytes 1572868
  463.5 84.6 %copy-start.8 = (f32[4096]{0:T(1024)S(1)}, f32[4096]{0:T(1024)}, u32[]{:S(2)}) copy-start(f32[4096]{0:T(1024)} %param.28) | copy-start | bytes 49156
Sparse Core Ops, SparseCore 0:
  154.5 80.9 all-reduce.3
  265.1 48.9 all-gather.1
  365.8 81.1 all-reduce.5
  463.6 84.4 reduce-scatter.1
